TPU v7x, 256 devices: a whole 4x4x8 slice. The times are simulated.
256 devices in a mesh: frame: 64 (over y, x_lo, z), patch: 4 (over x_hi, core).
Axes of the slice: x: 4 (x_hi: 2, x_lo: 2; x = x_hi * 2 + x_lo), y: 4, z: 8, core: 2. Of those that a mesh axis runs over, the one named last changes fastest.
Arguments:
- sky_image: float32 [64, 512, 1024], P('frame', None, 'patch'), may hold values from 0.5 to 1.5
- coefficients: float32 [64, 32, 64], P('frame', 'patch'), may hold values from -0.9 to 0.9
- mode_basis: float32 [64, 20736], replicated, may hold values from -6 to 6
- aperture: int32 [144, 144], replicated, may hold values from 0 to 1, as said below
Outputs:
- mode_gradient: float32 [64, 32, 64], P('frame', 'patch')
- object_spectrum: float32 [32, 2, 20736], P('patch', None, 'frame')
Inputs may be any that keep to these rules, and one draw needn't show every extreme that they name: `aperture`: 0 outside an annulus centred at (72, 72) with outer radius between 28 and 36 pixels and a central obstruction; inside it, each pixel is 1 except for randomly placed dead pixels, which are 0.
All inputs are finite; a program needn't handle non-finite values.
Results may differ from a plain program's by a relative error of at most 0.0003.
Values sent between devices are 32-bit elements; how exact they have to be, the bound alone decides.
A program may use at most 128 MiB of HBM per device.

v0:
```python
import math
import jax
import jax.numpy as jnp
from jax import lax
from jax.sharding import PartitionSpec as P

P_SIZE = 144
RIM = 8
reg_weight = 0.02
highest = lax.Precision.HIGHEST


def padded_2(array, sides, width):
    for axis, dim in sides:
        size, length = (lax.axis_size(axis), array.shape[dim])
        up = [(i, (i + 1) % size) for i in range(size - 1)]
        down = [(j, i) for i, j in up]
        last = lax.slice_in_dim(array, length - width, length, axis=dim)
        initial = lax.slice_in_dim(array, 0, width, axis=dim)
        before = lax.ppermute(last, axis, up)
        after = lax.ppermute(initial, axis, down)
        array = jnp.concatenate([before, array, after], axis=dim)
    return array


def window_table():
    offsets = jnp.arange(P_SIZE, dtype=jnp.float32)
    distance = jnp.minimum(offsets, P_SIZE - 1 - offsets)
    taper_value = 0.3 + 0.7 * jnp.sin(math.pi * (distance + 1.0) / (2.0 * (RIM + 1))) ** 2
    profile = jnp.where(distance < RIM, taper_value, 1.0)
    return profile[:, None] * profile[None, :]


def fourier_tables():
    position = jnp.arange(P_SIZE, dtype=jnp.int32)
    product = position[:, None] * position[None, :] % P_SIZE
    angles = 2.0 * math.pi / P_SIZE * product.astype(jnp.float32)
    return (jnp.cos(angles), jnp.sin(angles))


def left_mult(table, field_stack):
    return jnp.einsum("ab,fpbc->fpac", table, field_stack, precision=highest)


def right_mult(field_stack, table):
    return jnp.einsum("fpab,bc->fpac", field_stack, table, precision=highest)


def transform(real_part, imag_part, tables):
    cosine_table, sine_table = tables
    if imag_part is None:
        left_real = left_mult(cosine_table, real_part)
        left_imag = -left_mult(sine_table, real_part)
    else:
        left_real = left_mult(cosine_table, real_part) + left_mult(sine_table, imag_part)
        left_imag = left_mult(cosine_table, imag_part) - left_mult(sine_table, real_part)
    out_real = right_mult(left_real, cosine_table) + right_mult(left_imag, sine_table)
    out_imag = right_mult(left_imag, cosine_table) - right_mult(left_real, sine_table)
    return (out_real, out_imag)


def body(sky_image, coefficients, mode_basis, aperture):
    frames_here, row_total, column_total = sky_image.shape
    patches_here = coefficients.shape[1]
    tile_side = P_SIZE - 2 * RIM
    tables = fourier_tables()
    window = window_table()
    widened = padded_2(sky_image, (("patch", 2),), RIM)
    padded = jnp.pad(widened, ((0, 0), (RIM, RIM), (0, 0)))
    row_count = row_total // tile_side
    column_count = column_total // tile_side
    blocks = []
    for column_place in range(column_count):
        for row_place in range(row_count):
            blocks.append(
                padded[
                    :,
                    row_place * tile_side : row_place * tile_side + P_SIZE,
                    column_place * tile_side : column_place * tile_side + P_SIZE,
                ]
            )
    patches = jnp.stack(blocks, axis=1)
    data_real, data_imag = transform(window * patches, None, tables)
    data_real = data_real / P_SIZE
    data_imag = data_imag / P_SIZE
    pupil_mask = aperture.astype(jnp.float32)
    pupil_area = jnp.sum(pupil_mask)

    def transfer_map(mode_weights):
        phase_map = jnp.einsum("fpk,kx->fpx", mode_weights, mode_basis, precision=highest).reshape(
            frames_here, patches_here, P_SIZE, P_SIZE
        )
        focal_real, focal_imag = transform(
            pupil_mask * jnp.cos(phase_map), pupil_mask * jnp.sin(phase_map), tables
        )
        intensity = (focal_real**2 + focal_imag**2) / (P_SIZE * P_SIZE * pupil_area)
        return transform(intensity, None, tables)

    (otf_real, otf_imag), pullback = jax.vjp(transfer_map, coefficients)
    numer_real = jnp.sum(otf_real * data_real + otf_imag * data_imag, axis=0)
    numer_imag = jnp.sum(otf_real * data_imag - otf_imag * data_real, axis=0)
    power = jnp.sum(otf_real**2 + otf_imag**2, axis=0)
    spectra = jnp.stack([numer_real, numer_imag, power], axis=1).reshape(
        patches_here, 3, P_SIZE * P_SIZE
    )
    frame_total = frames_here * lax.axis_size("frame")
    damping = reg_weight * frame_total
    share = P_SIZE * P_SIZE // lax.axis_size("frame")
    totals = lax.psum(spectra, "frame")
    denominator = totals[:, 2] + damping
    estimate = totals[:, 0:2] / denominator[:, None]
    own_part = lax.dynamic_slice_in_dim(estimate, lax.axis_index("frame") * share, share, 2)
    object_real = estimate[:, 0].reshape(patches_here, P_SIZE, P_SIZE)[None]
    object_imag = estimate[:, 1].reshape(patches_here, P_SIZE, P_SIZE)[None]
    error_real = data_real - (object_real * otf_real - object_imag * otf_imag)
    error_imag = data_imag - (object_real * otf_imag + object_imag * otf_real)
    scale_factor = 2.0 / (P_SIZE * P_SIZE)
    cotangent_real = -scale_factor * (error_real * object_real + error_imag * object_imag)
    cotangent_imag = scale_factor * (error_real * object_imag - error_imag * object_real)
    gradient = pullback((cotangent_real, cotangent_imag))[0]
    mode_total = lax.psum(jnp.sum(gradient, axis=0), "frame")
    mode_gradient = gradient - mode_total[None] / frame_total
    return (mode_gradient, own_part)


def solution(mesh):
    in_specs = (P("frame", None, "patch"), P("frame", "patch", None), P(), P())
    out_specs = (P("frame", "patch", None), P("patch", None, "frame"))
    return jax.shard_map(body, mesh=mesh, in_specs=in_specs, out_specs=out_specs, check_vma=False)
```

profile of v0, /device:TPU:4, one launch (start us, length us, event | category | flops | bytes accessed | tf_op | source)
XLA Modules:
  0.0 938.4 jit_solution(11270163691090871212)
XLA Ops:
  11.1 5.1 collective-permute-start.1
  18.0 6.6 fusion.345
  41.0 3.2 fusion.86
  44.2 3.2 convolution_add_fusion.8
  47.4 3.2 convolution_subtract_fusion.2
  51.2 3.3 fusion
  54.5 3.4 convolution_bitcast_fusion
  58.0 3.2 fusion.83
  61.2 3.2 fusion.81
  64.4 3.2 convolution_add_fusion.7
  70.7 3.2 convolution_bitcast_fusion.1
  73.9 3.2 fusion.1
  80.3 3.2 fusion.79
  83.5 3.6 fusion.19
  87.1 3.2 fusion.16
  90.3 5.7 multiply_add_fusion.1
  119.0 597.5 %all-reduce.3.cloned.1.call-done = f32[8,3,20736]{2,0,1:T(8,128)} async-done(((f32[8,3,20736]{2,0,1:T(8,128)}), f32[8,3,20736]{2,0,1:T(8,128)}) %all-reduce.3.cloned.1.call-update) | async-done | bytes 1990672 | tf_op jit(solution)/shard_map/psum | solution.py:109
  726.6 3.3 add_multiply_fusion
  736.6 3.4 fusion.58
  740.0 3.2 fusion.12
  748.9 3.6 fusion.22
  760.5 3.2 fusion.6
  765.1 6.1 fusion.347
  771.2 158.1 %psum.15 = f32[8,64]{1,0:T(8,128)S(1)} all-reduce(f32[8,64]{1,0:T(8,128)S(1)} %fusion.347), channel_id=1, replica_groups=mesh['frame'=64,'patch'=4] {'frame'}, use_global_device_ids=true, to_apply=%region_2.3 | all-reduce | flops 512 | bytes 4096 | tf_op jit(solution)/shard_map/psum | solution.py:121
  (89 shorter events, 85.0 us)
Async XLA Ops:
  7.2 10.8 %copy-start = (f32[1,8,64]{2,1,0:T(8,128)S(1)}, f32[1,8,64]{2,1,0:T(8,128)}, u32[]{:S(2)}) copy-start(f32[1,8,64]{2,1,0:T(8,128)} %param.5) | copy-start | bytes 6148
  7.2 10.0 %copy-start.13 = (s32[144,144]{1,0:T(8,128)S(1)}, s32[144,144]{1,0:T(8,128)}, u32[]{:S(2)}) copy-start(s32[144,144]{1,0:T(8,128)} %param.7) | copy-start | bytes 248836
  7.2 709.4 %all-reduce.3.cloned.1.call-start = ((), (), s32[]{:S(2)}) async-start(), calls=%async_computation | async-start | bytes 3981312 | tf_op jit(solution)/shard_map/psum | solution.py:109
  9.2 58.5 %collective-permute-start = (f32[1,512,8]{2,1,0:T(8,128)}, f32[1,512,8]{2,1,0:T(8,128)S(1)}, u32[]{:S(2)}, u32[]{:S(2)}) collective-permute-start(f32[1,512,8]{2,1,0:T(8,128)} %get-tuple-element.13), channel_id=1, source_target_pairs={{0,1},{1,2},{2,3},{4,5},{5,6},{6,7},{8,9},{9,10},{10,11},{12,13},{... | collective-permute-start | bytes 49160 | tf_op jit(solution)/shard_map/ppermute | solution.py:20
  11.1 56.6 %collective-permute-start.1 = (f32[1,512,8]{2,1,0:T(8,128)}, f32[1,512,8]{2,1,0:T(8,128)}, u32[]{:S(2)}, u32[]{:S(2)}) collective-permute-start(f32[1,512,8]{2,1,0:T(8,128)} %get-tuple-element.14), channel_id=1, source_target_pairs={{1,0},{2,1},{3,2},{5,4},{6,5},{7,6},{9,8},{10,9},{11,10},{13,12},{... | collective-permute-start | bytes 49160 | tf_op jit(solution)/shard_map/ppermute | solution.py:21
  18.0 20.9 %copy-start.6 = (f32[144,144]{0,1:T(8,128)}, f32[144,144]{0,1:T(8,128)S(1)}, u32[]{:S(2)}) copy-start(f32[144,144]{0,1:T(8,128)S(1)} %copy.38) | copy-start | bytes 248836
  24.6 0.9 copy-start.9
  24.6 2.3 copy-start.8
  47.4 7.1 copy-start.4
  64.4 3.3 copy-start.2
  90.3 5.7 copy-start.3
  719.1 1.5 copy-start.10
  745.5 1.7 copy-start.5
  755.6 1.7 copy-start.7
  755.6 1.7 copy-start.12
  757.3 3.2 copy-start.11
  765.1 166.3 %copy-start.1 = (f32[1,8,64]{2,1,0:T(8,128)S(1)}, f32[1,8,64]{2,1,0:T(8,128)}, u32[]{:S(2)}) copy-start(f32[1,8,64]{2,1,0:T(8,128)} %param.5) | copy-start | bytes 6148
Sparse Core Ops, SparseCore 0:
  107.2 609.3 all-reduce.2
where the time goes:
time: 949 us; the launch traced here: 938 us
  waiting for transfers between devices  598 us (63%)
  blocking collectives  158 us (17%)
  matrix products  107 us (11%)
  local copies, waits for them, and re-layouts  40.5 us (4%)
  between operations  15.4 us (2%)
  other arithmetic  12.6 us (1%)
    psum x1, waiting for transfers between devices, body(): totals = lax.psum(spectra, 'frame')  598 us
    psum x1, blocking collectives, body(): mode_total = lax.psum(jnp.sum(gradient, axis=0), 'frame')  158 us
    dot_general x20, matrix products, right_mult(): return jnp.einsum('fpab,bc->fpac', field_stack, table, precision=highest)  54.5 us
    dot_general x14, matrix products, left_mult(): return jnp.einsum('ab,fpbc->fpac', table, field_stack, precision=highest)  40 us
  transfers between devices with their start and end apart: 3, of which 1 were waited for; matrix products, arithmetic and copies ran while one was open for 7% of the time, Pallas kernels for 0%

commit v1 on v0

--- a/solution.py
+++ b/solution.py
@@ -118,7 +118,7 @@
     cotangent_real = -scale_factor * (error_real * object_real + error_imag * object_imag)
     cotangent_imag = scale_factor * (error_real * object_imag - error_imag * object_real)
     gradient = pullback((cotangent_real, cotangent_imag))[0]
-    mode_total = lax.psum(jnp.sum(gradient, axis=0), "frame")
+    mode_total = jnp.sum(lax.all_gather(jnp.sum(gradient, axis=0), "frame"), axis=0)
     mode_gradient = gradient - mode_total[None] / frame_total
     return (mode_gradient, own_part)
 

time: 949 us -> 948 us (level)
    psum x1 -> x0, blocking collectives: 158 us -> none  [body(): mode_total = lax.psum(jnp.sum(gradient, axis=0), 'frame')]
    all_gather x0 -> x1, blocking collectives: none -> 157 us  [body(): lax.all_gather(jnp.sum(gradient, axis=0), 'frame')]
where the time goes in v1:
time: 948 us; the launch traced here: 938 us
  waiting for transfers between devices  597 us (63%)
  blocking collectives  157 us (17%)
  matrix products  106 us (11%)
  local copies, waits for them, and re-layouts  40.3 us (4%)
  between operations  15.4 us (2%)
  other arithmetic  14.5 us (2%)
    psum x1, waiting for transfers between devices, body(): totals = lax.psum(spectra, 'frame')  597 us
    all_gather x1, blocking collectives, body(): lax.all_gather(jnp.sum(gradient, axis=0), 'frame')  157 us
    dot_general x20, matrix products, right_mult(): return jnp.einsum('fpab,bc->fpac', field_stack, table, precision=highest)  53.8 us
    dot_general x14, matrix products, left_mult(): return jnp.einsum('ab,fpbc->fpac', table, field_stack, precision=highest)  39.9 us
  transfers between devices with their start and end apart: 3, of which 1 were waited for; matrix products, arithmetic and copies ran while one was open for 7% of the time, Pallas kernels for 0%

profile of v1, /device:TPU:4, one launch (start us, length us, event | category | flops | bytes accessed | tf_op | source)
XLA Modules:
  0.0 937.5 jit_solution(2380939509024498990)
XLA Ops:
  11.1 5.1 collective-permute-start.1
  18.0 6.6 fusion.345
  44.1 3.1 convolution_add_fusion.8
  51.0 3.2 fusion
  54.2 3.4 convolution_bitcast_fusion
  57.7 3.2 fusion.83
  60.9 3.2 fusion.81
  64.1 3.1 convolution_add_fusion.7
  72.2 3.2 convolution_bitcast_fusion.1
  75.4 3.2 fusion.1
  81.7 3.5 fusion.79
  85.2 3.1 fusion.19
  88.3 3.2 fusion.16
  91.5 5.6 multiply_add_fusion.1
  111.2 3.1 sin.71
  120.2 596.9 %all-reduce.3.cloned.1.call-done = f32[8,3,20736]{2,0,1:T(8,128)} async-done(((f32[8,3,20736]{2,0,1:T(8,128)}), f32[8,3,20736]{2,0,1:T(8,128)}) %all-reduce.3.cloned.1.call-update) | async-done | bytes 1990672 | tf_op jit(solution)/shard_map/psum | solution.py:109
  736.9 3.3 fusion.58
  740.2 3.1 fusion.12
  749.0 3.6 fusion.22
  752.6 3.2 fusion.20
  757.5 3.2 fusion.9
  760.7 3.3 fusion.6
  765.3 6.1 fusion.347
  771.4 156.9 %all-gather = f32[512,64]{1,0:T(8,128)S(1)} all-gather(f32[8,64]{1,0:T(8,128)S(1)} %fusion.347), channel_id=2, replica_groups=mesh['frame'=64,'patch'=4] {'frame'}, dimensions={0}, use_global_device_ids=true | all-gather | bytes 133120 | tf_op jit(solution)/shard_map/all_gather | solution.py:121
  (90 shorter events, 86.5 us)
Async XLA Ops:
  7.2 10.8 %copy-start = (f32[1,8,64]{2,1,0:T(8,128)S(1)}, f32[1,8,64]{2,1,0:T(8,128)}, u32[]{:S(2)}) copy-start(f32[1,8,64]{2,1,0:T(8,128)} %param.5) | copy-start | bytes 6148
  7.2 10.0 %copy-start.13 = (s32[144,144]{1,0:T(8,128)S(1)}, s32[144,144]{1,0:T(8,128)}, u32[]{:S(2)}) copy-start(s32[144,144]{1,0:T(8,128)} %param.7) | copy-start | bytes 248836
  7.2 709.9 %all-reduce.3.cloned.1.call-start = ((), (), s32[]{:S(2)}) async-start(), calls=%async_computation | async-start | bytes 3981312 | tf_op jit(solution)/shard_map/psum | solution.py:109
  9.2 58.1 %collective-permute-start = (f32[1,512,8]{2,1,0:T(8,128)}, f32[1,512,8]{2,1,0:T(8,128)}, u32[]{:S(2)}, u32[]{:S(2)}) collective-permute-start(f32[1,512,8]{2,1,0:T(8,128)} %get-tuple-element.13), channel_id=1, source_target_pairs={{0,1},{1,2},{2,3},{4,5},{5,6},{6,7},{8,9},{9,10},{10,11},{12,13},{... | collective-permute-start | bytes 49160 | tf_op jit(solution)/shard_map/ppermute | solution.py:20
  11.1 56.2 %collective-permute-start.1 = (f32[1,512,8]{2,1,0:T(8,128)}, f32[1,512,8]{2,1,0:T(8,128)}, u32[]{:S(2)}, u32[]{:S(2)}) collective-permute-start(f32[1,512,8]{2,1,0:T(8,128)} %get-tuple-element.14), channel_id=1, source_target_pairs={{1,0},{2,1},{3,2},{5,4},{6,5},{7,6},{9,8},{10,9},{11,10},{13,12},{... | collective-permute-start | bytes 49160 | tf_op jit(solution)/shard_map/ppermute | solution.py:21
  18.0 20.8 %copy-start.6 = (f32[144,144]{0,1:T(8,128)}, f32[144,144]{0,1:T(8,128)S(1)}, u32[]{:S(2)}) copy-start(f32[144,144]{0,1:T(8,128)S(1)} %copy.38) | copy-start | bytes 248836
  24.6 0.9 copy-start.9
  24.6 2.3 copy-start.8
  47.2 7.0 copy-start.4
  64.0 3.2 copy-start.2
  91.5 5.6 copy-start.3
  719.7 1.5 copy-start.10
  745.6 1.7 copy-start.5
  755.8 1.7 copy-start.7
  755.8 1.7 copy-start.12
  757.5 3.2 copy-start.11
  765.3 165.2 %copy-start.1 = (f32[1,8,64]{2,1,0:T(8,128)S(1)}, f32[1,8,64]{2,1,0:T(8,128)}, u32[]{:S(2)}) copy-start(f32[1,8,64]{2,1,0:T(8,128)} %param.5) | copy-start | bytes 6148
Sparse Core Ops, SparseCore 0:
  108.3 608.7 all-reduce.2
